TPU v7x, 128 devices: a whole 4x4x4 slice. The times are simulated.
128 devices in a mesh: dp: 16 (over x_lo, z, core), tensor: 8 (over y, x_hi).
Axes of the slice: x: 4 (x_hi: 2, x_lo: 2; x = x_hi * 2 + x_lo), y: 4, z: 4, core: 2. Of those that a mesh axis runs over, the one named last changes fastest.
Arguments:
- out_grad: bfloat16 [4096, 4096], P('dp'), may hold values from -8 to 8
- hidden_act: bfloat16 [4096, 15360], P('dp', 'tensor'), may hold values from -6 to 6
- log_ratio: float32 [128], P('dp'), may hold values from -40 to 40
- pair_order: int32 [16, 8], P('dp'), may hold values from 0 to 7, each once within a row
- seq_len: int32 [128], P('dp'), may hold values from 1 to 32, 2560 in all
- master: float32 [4096, 15360], P('dp', 'tensor'), may hold values from -0.046875 to 0.046875
- moment: float32 [4096, 15360], P('dp', 'tensor'), may hold values from -6 to 6
- second: float32 [4096, 15360], P('dp', 'tensor'), may hold values from 0.005 to 0.08
- next_act: bfloat16 [8192, 15360], P('dp', 'tensor'), may hold values from -6 to 6
Outputs:
- new_master: float32 [4096, 15360], P('dp', 'tensor')
- new_moment: float32 [4096, 15360], P('dp', 'tensor')
- new_second: float32 [4096, 15360], P('dp', 'tensor')
- update: float32 [4096, 15360], P('dp', 'tensor')
- next_out: bfloat16 [8192, 4096], P('dp', 'tensor')
Inputs may be any that keep to these rules, and one draw needn't show every extreme that they name: Each row of pair_order holds every number below 8 once.
All inputs are finite; a program needn't handle non-finite values. No bound on the sum of `seq_len` on one device may be relied on, other than what follows from the above.
Results may differ from a plain program's by a relative error of at most 0.02.
Values may be sent and summed in bfloat16 or wider, within the bound.
A program may use at most 128 MiB of HBM per device.

v0:
```python
import jax
import jax.numpy as jnp
from jax import lax
from jax.sharding import PartitionSpec as P

LEN = 32


beta_dpo = 0.1
beta_one = 0.9
beta_two = 0.999
bias_one = 1.0 - 0.9**10
bias_two = 1.0 - 0.999**10
adam_eps = 1e-08
rate_learn = 0.001


def row_factors(ratios, pair_row, lengths):
    seq_count = ratios.shape[0]
    seq_slots = jnp.arange(seq_count, dtype=jnp.int32)
    chosen = pair_row[0::2]
    rejected = pair_row[1::2]
    pick_chosen = (chosen[:, None] == seq_slots[None, :]).astype(jnp.float32)
    pick_rejected = (rejected[:, None] == seq_slots[None, :]).astype(jnp.float32)
    margin = beta_dpo * (
        jnp.sum(pick_chosen * ratios[None, :], axis=1)
        - jnp.sum(pick_rejected * ratios[None, :], axis=1)
    )
    weight = beta_dpo * jax.nn.sigmoid(-margin)
    coefficient = jnp.sum(weight[:, None] * (pick_rejected - pick_chosen), axis=0)
    position = jnp.arange(LEN, dtype=jnp.int32)
    in_length = (position[None, :] < lengths[:, None]).astype(jnp.float32)
    return coefficient[:, None] * in_length


def body(out_grad, hidden_act, log_ratio, pair_order, seq_len, master, moment, second, next_act):
    factors = row_factors(log_ratio, pair_order[0], seq_len)
    scaled = (out_grad.astype(jnp.float32) * factors.reshape(-1)[:, None]).astype(jnp.bfloat16)
    grad = lax.psum_scatter(
        lax.dot_general(
            scaled, hidden_act, (((0,), (0,)), ((), ())), preferred_element_type=jnp.float32
        ).astype(jnp.bfloat16),
        "dp",
        scatter_dimension=0,
        tiled=True,
    ).astype(jnp.float32)
    new_moment = beta_one * moment + (1.0 - beta_one) * grad
    new_second = beta_two * second + (1.0 - beta_two) * grad * grad
    update = new_moment / bias_one / (jnp.sqrt(new_second / bias_two) + adam_eps)
    new_master = master - rate_learn * update
    weights = new_master.astype(jnp.bfloat16)
    partial_next = lax.dot_general(
        next_act,
        lax.all_gather(weights, "dp", axis=0, tiled=True),
        (((1,), (1,)), ((), ())),
        preferred_element_type=jnp.float32,
    )
    summed = lax.psum_scatter(
        partial_next.astype(jnp.bfloat16), "tensor", scatter_dimension=1, tiled=True
    )
    return (new_master, new_moment, new_second, update, summed)


def solution(mesh):
    return jax.shard_map(
        body,
        mesh=mesh,
        in_specs=(
            P("dp", None),
            P("dp", "tensor"),
            P("dp"),
            P("dp", None),
            P("dp"),
            P("dp", "tensor"),
            P("dp", "tensor"),
            P("dp", "tensor"),
            P("dp", "tensor"),
        ),
        out_specs=(
            P("dp", "tensor"),
            P("dp", "tensor"),
            P("dp", "tensor"),
            P("dp", "tensor"),
            P("dp", "tensor"),
        ),
        check_vma=False,
    )
```

profile of v0, /device:TPU:0, one launch (start us, length us, event | category | flops | bytes accessed | tf_op | source)
XLA Modules:
  0.0 319.7 jit_solution(7468882576151376659)
XLA Ops:
  7.2 0.0 copy-start
  7.2 0.0 reduce-scatter.3.cloned.1.call-start
  7.2 0.9 slice.7
  8.1 0.7 slice.6
  8.8 0.9 select_reduce_fusion
  9.7 0.1 multiply_reduce_fusion
  9.8 0.7 fusion.4
  10.6 0.1 mul.92
  10.6 12.0 %convolution_convert_fusion = bf16[4096,1920]{1,0:T(8,128)(2,1)} fusion(bf16[256,1920]{1,0:T(8,128)(2,1)} %param.10, bf16[256,4096]{1,0:T(8,128)(2,1)} %param.9, f32[256]{0:T(256)S(1)} %mul.92), kind=kOutput, calls=%fused_computation | convolution fusion | flops 4037541888 | bytes 18809856 | tf_op jit(solution)/shard_map/dot_general | solution.py:40
  22.6 0.0 reduce-scatter.3.cloned.1.call-update
  22.7 0.0 all-gather.2.cloned.1.call-start
  22.7 95.8 %reduce-scatter.3.cloned.1.call-done = bf16[256,1920]{1,0:T(8,128)(2,1)} async-done(((bf16[4096,1920]{1,0:T(8,128)(2,1)}), bf16[256,1920]{1,0:T(8,128)(2,1)}) %reduce-scatter.3.cloned.1.call-update) | async-done | bytes 983056 | tf_op jit(solution)/shard_map/reduce_scatter | solution.py:39
  118.5 7.7 %fusion.5 = (bf16[256,1920]{1,0:T(8,128)(2,1)}, f32[256,1920]{1,0:T(8,128)}, f32[256,1920]{1,0:T(8,128)}, f32[256,1920]{1,0:T(8,128)}, f32[256,1920]{1,0:T(8,128)}) fusion(f32[256,1920]{1,0:T(8,128)} %param.14, bf16[256,1920]{1,0:T(8,128)(2,1)} %reduce-scatter.3.cloned.1.call-done, f32[256,1920]{1,0:T(8,128)} %param.15, f32[256,1920]{1,0:T(8,128)} %param.16), kind=kLoop, calls=%fused_computation.19 | loop fusion | flops 7372800 | bytes 15728640 | tf_op jit(solution)/shard_map/convert_element_type | solution.py:51
  126.1 0.0 all-gather.2.cloned.1.call-update
  126.2 0.0 reduce-scatter.5.cloned.1.call-start
  126.2 85.7 %all-gather.2.cloned.1.call-done = bf16[4096,1920]{1,0:T(8,128)(2,1)} async-done(((bf16[256,1920]{1,0:T(8,128)(2,1)}), bf16[4096,1920]{1,0:T(8,128)(2,1)}) %all-gather.2.cloned.1.call-update) | async-done | bytes 15728656 | tf_op jit(solution)/shard_map/all_gather | solution.py:54
  211.9 0.0 copy-done
  211.9 13.7 %fusion = bf16[512,4096]{0,1:T(8,128)(2,1)} fusion(bf16[4096,1920]{1,0:T(8,128)(2,1)} %all-gather.2.cloned.1.call-done, bf16[512,1920]{1,0:T(8,128)(2,1)S(1)} %copy-done), kind=kOutput, calls=%fused_computation.2 | convolution fusion | flops 8055160832 | bytes 21889024 | tf_op jit(solution)/shard_map/dot_general | solution.py:52
  225.6 0.0 reduce-scatter.5.cloned.1.call-update
  225.7 85.5 %reduce-scatter.5.cloned.1.call-done = bf16[512,512]{0,1:T(8,128)(2,1)} async-done(((bf16[512,4096]{0,1:T(8,128)(2,1)}), bf16[512,512]{0,1:T(8,128)(2,1)}) %reduce-scatter.5.cloned.1.call-update) | async-done | bytes 524304 | tf_op jit(solution)/shard_map/reduce_scatter | solution.py:58
  311.1 2.0 copy.15
  (1 shorter events, 0.0 us)
Async XLA Ops:
  7.2 204.7 %copy-start = (bf16[512,1920]{1,0:T(8,128)(2,1)S(1)}, bf16[512,1920]{1,0:T(8,128)(2,1)}, u32[]{:S(2)}) copy-start(bf16[512,1920]{1,0:T(8,128)(2,1)} %param.17) | copy-start | bytes 5898244
  7.2 111.3 %reduce-scatter.3.cloned.1.call-start = ((), (), s32[]{:S(2)}) async-start(), calls=%async_computation.2 | async-start | bytes 16711680 | tf_op jit(solution)/shard_map/reduce_scatter | solution.py:39
  22.7 189.2 %all-gather.2.cloned.1.call-start = ((), (), s32[]{:S(2)}) async-start(), calls=%async_computation.3 | async-start | bytes 16711680 | tf_op jit(solution)/shard_map/all_gather | solution.py:54
  126.2 185.0 %reduce-scatter.5.cloned.1.call-start = ((), (), s32[]{:S(2)}) async-start(), calls=%async_computation.4 | async-start | bytes 4718592 | tf_op jit(solution)/shard_map/reduce_scatter | solution.py:58
Sparse Core Ops, SparseCore 0:
  22.8 95.6 reduce-scatter.2
  126.3 85.5 all-gather.1
  225.8 85.2 reduce-scatter.4
where the time goes:
time: 320 us
  waiting for transfers between devices  267 us (83%)
  matrix products  25.7 us (8%)
  between operations  13.8 us (4%)
  other arithmetic  9.36 us (3%)
  local copies, waits for them, and re-layouts  3.75 us (1%)
    reduce_scatter x1, waiting for transfers between devices, body(): lax.psum_scatter(lax.dot_general(scaled, hidden_act, (((0,), (0,)), ((),...  95.8 us
    all_gather x1, waiting for transfers between devices, body(): lax.all_gather(weights, 'dp', axis=0, tiled=True)  85.7 us
    reduce_scatter x1, waiting for transfers between devices, body(): lax.psum_scatter(partial_next.astype(jnp.bfloat16), 'tensor', scatter_dim...  85.5 us
    dot_general x1, matrix products, body(): lax.dot_general(next_act, lax.all_gather(weights, 'dp', axis=0, tiled=Tru...  13.7 us
    dot_general x1, matrix products, body(): lax.dot_general(scaled, hidden_act, (((0,), (0,)), ((), ())), preferred_e...  12 us
    convert_element_type x1, other arithmetic, body(): weights = new_master.astype(jnp.bfloat16)  7.65 us
  transfers between devices with their start and end apart: 3, of which 3 were waited for; matrix products, arithmetic and copies ran while one was open for 0% of the time, Pallas kernels for 0%

commit v1 on v0

v1 whole, which is shorter than its diff:
```python
import jax
import jax.numpy as jnp
from jax import lax
from jax.experimental import pallas as pl
from jax.experimental.pallas import tpu as pltpu
from jax.sharding import PartitionSpec as P

LEN = 32
beta_dpo = 0.1
beta_one = 0.9
beta_two = 0.999
bias_one = 1.0 - 0.9**10
bias_two = 1.0 - 0.999**10
adam_eps = 1e-08
rate_learn = 0.001

MESH = pl.DeviceIdType.MESH
F32 = jnp.float32
BF16 = jnp.bfloat16

FL = 1920
BLK = 256
HALF = 128
CHUNKS = ((0, 768), (768, 768), (1536, 384))
EVENTS = ((0, 0), (0, 1), (1, 0), (3, 0), (1, 1), (3, 1), (2, 0), (2, 1))


def mod4(v):
    return lax.rem(v + 8, 4)


def kernel(
    og_hbm, hid_hbm, ratio_ref, pair_ref, len_ref, mas_hbm, mom_hbm, sec_hbm, nact_hbm,
    mas_out, mom_out, sec_out, upd_out, next_out,
    H, SC, ST, SS, OG, ACC, RSS, RSR, MAS, MOM, SEC, WB, NA, XS, XB, YS, YB, NO,
    loc_sem,
    ha_s, ha_r, sa_s, sa_r, sb_s, sb_r, rs_s, rs_r, na_s, na_r, w_s, w_r, x_s, x_r, y_s, y_r,
):
    dp = lax.axis_index("dp")
    tn = lax.axis_index("tensor")
    xl = dp // 8
    z = lax.rem(dp // 2, 4)
    c = lax.rem(dp, 2)
    y = tn // 2
    xh = lax.rem(tn, 2)

    def dev(xl_=None, z_=None, c_=None, y_=None, xh_=None):
        xl_ = xl if xl_ is None else xl_
        z_ = z if z_ is None else z_
        c_ = c if c_ is None else c_
        y_ = y if y_ is None else y_
        xh_ = xh if xh_ is None else xh_
        return (xl_ * 8 + z_ * 2 + c_, y_ * 2 + xh_)

    right, left, far = mod4(z + 1), mod4(z - 1), mod4(z + 2)
    pc = 1 - c

    barrier = pltpu.get_barrier_semaphore()
    for k in range(1, 16):
        idx = lax.rem(xl * 8 + tn + k, 16)
        pl.semaphore_signal(
            barrier, inc=1,
            device_id=((idx // 8) * 8 + z * 2 + c, lax.rem(idx, 8)), device_id_type=MESH)
    for k in range(1, 8):
        idx = lax.rem(z * 2 + c + k, 8)
        pl.semaphore_signal(
            barrier, inc=1, device_id=(xl * 8 + idx, tn), device_id_type=MESH)

    locals_ = []

    def local(src, dst):
        cp = pltpu.make_async_copy(src, dst, loc_sem.at[len(locals_)])
        cp.start()
        locals_.append(cp)
        return cp

    def aligned(v, m):
        return pl.multiple_of(v * m, m)

    qrows = pl.ds(aligned(y, 64), 64)
    og_cp = local(og_hbm.at[qrows, :], OG)
    own_h = local(hid_hbm, H.at[pl.ds(aligned(z * 2 + c, BLK), BLK), :])
    mas_cp = local(mas_hbm, MAS)
    mom_cp = local(mom_hbm, MOM)
    sec_cp = local(sec_hbm, SEC)
    own_na = local(nact_hbm, NA.at[xl])
    pl.semaphore_wait(barrier, 22)

    sends = []

    def remote(src, dst, ss, rs, to):
        return pltpu.make_async_remote_copy(
            src, dst, ss, rs, device_id=to, device_id_type=MESH)

    def send(src, dst, ss, rs, to):
        cp = remote(src, dst, ss, rs, to)
        cp.start()
        sends.append((None, cp))

    def arrived(dst, ss, rs):
        remote(dst, dst, ss, rs, (dp, tn)).wait_recv()

    def hrow(zz, cc, half=None):
        if half is None:
            return pl.ds(aligned(zz * 2 + cc, BLK), BLK)
        return pl.ds(pl.multiple_of((zz * 2 + cc) * BLK + half * HALF, HALF), HALF)

    def h_own(i):
        cs = pl.ds(CHUNKS[i][0], CHUNKS[i][1])
        src = hid_hbm.at[:, cs]
        dst = H.at[hrow(z, c), cs]
        b = i * 9
        send(src, dst, ha_s.at[b], ha_r.at[b], dev(z_=right))
        send(src, dst, ha_s.at[b + 1], ha_r.at[b + 1], dev(z_=left))
        send(src, dst, ha_s.at[b + 2], ha_r.at[b + 2], dev(c_=pc))

    def h_view(i, zz, cc, half=None):
        return H.at[hrow(zz, cc, half), pl.ds(CHUNKS[i][0], CHUNKS[i][1])]

    def h_forward_near(i):
        b = i * 9
        v = h_view(i, left, c)
        arrived(v, ha_s.at[b], ha_r.at[b])
        v0 = h_view(i, left, c, 0)
        send(v0, v0, ha_s.at[b + 5], ha_r.at[b + 5], dev(z_=right))
        send(v, v, ha_s.at[b + 3], ha_r.at[b + 3], dev(c_=pc))
        v = h_view(i, right, c)
        arrived(v, ha_s.at[b + 1], ha_r.at[b + 1])
        v1 = h_view(i, right, c, 1)
        send(v1, v1, ha_s.at[b + 6], ha_r.at[b + 6], dev(z_=left))
        send(v, v, ha_s.at[b + 4], ha_r.at[b + 4], dev(c_=pc))

    def h_forward_far(i):
        b = i * 9
        for half in (0, 1):
            v = h_view(i, far, c, half)
            arrived(v, ha_s.at[b + 5 + half], ha_r.at[b + 5 + half])
            send(v, v, ha_s.at[b + 7 + half], ha_r.at[b + 7 + half], dev(c_=pc))

    def h_rest(i):
        b = i * 9
        arrived(h_view(i, z, pc), ha_s.at[b + 2], ha_r.at[b + 2])
        arrived(h_view(i, left, pc), ha_s.at[b + 3], ha_r.at[b + 3])
        arrived(h_view(i, right, pc), ha_s.at[b + 4], ha_r.at[b + 4])
        for half in (0, 1):
            arrived(h_view(i, far, pc, half), ha_s.at[b + 7 + half], ha_r.at[b + 7 + half])

    def na_send(p):
        rows = pl.ds(p * HALF, HALF)
        send(nact_hbm.at[rows, :], NA.at[xl, rows, :], na_s.at[p], na_r.at[p], dev(xl_=1 - xl))

    h_own(0)
    na_send(0)
    na_send(1)

    lane = lax.broadcasted_iota(jnp.int32, (1, 8), 1)
    ratios = ratio_ref[...]
    coef = jnp.zeros((1, 8), F32)
    for p in range(4):
        oc = (lane == pair_ref[0, 2 * p]).astype(F32)
        orj = (lane == pair_ref[0, 2 * p + 1]).astype(F32)
        margin = beta_dpo * (
            jnp.sum(oc * ratios, axis=1, keepdims=True)
            - jnp.sum(orj * ratios, axis=1, keepdims=True))
        weight = beta_dpo * jax.nn.sigmoid(-margin)
        coef = coef + weight * (orj - oc)
    row = lax.broadcasted_iota(jnp.int32, (64, 8), 0)
    lane64 = lax.broadcasted_iota(jnp.int32, (64, 8), 1)
    upper = (row >= LEN).astype(jnp.int32)
    sel = (lane64 == 2 * y + upper).astype(F32)
    row_coef = jnp.sum(sel * coef, axis=1, keepdims=True)
    row_len = jnp.sum(sel * len_ref[...].astype(F32), axis=1, keepdims=True)
    pos = (row - LEN * upper)[:, 0:1].astype(F32)
    factor = row_coef * (pos < row_len).astype(F32)
    og_cp.wait()
    for dz in range(4):
        for dc in range(2):
            zz = mod4(z + dz)
            cc = c if dc == 0 else pc
            k = dz * 2 + dc
            for b in range(2):
                cols = pl.ds(pl.multiple_of((b * 8 + zz * 2 + cc) * BLK, BLK), BLK)
                SS[k, :, b * BLK:(b + 1) * BLK] = (OG[:, cols].astype(F32) * factor).astype(BF16)
            dst = SC.at[z * 2 + c, qrows, :]
            if k == 0:
                SC[z * 2 + c, qrows, :] = SS[0]
            else:
                send(SS.at[k], dst, sa_s.at[k], sa_r.at[k], dev(z_=zz, c_=cc))
    h_own(1)
    for dz in range(4):
        for dc in range(2):
            k = dz * 2 + dc
            if k:
                zz = mod4(z - dz)
                cc = c if dc == 0 else pc
                arrived(SC.at[zz * 2 + cc, qrows, :], sa_s.at[k], sa_r.at[k])
    for dy in (1, 3, 2):
        v = SC.at[:, qrows, :]
        send(v, v, sb_s.at[dy], sb_r.at[dy], dev(y_=mod4(y + dy)))

    h_forward_near(0)
    h_own(2)

    for dy in (1, 3, 2):
        yy = mod4(y - dy)
        arrived(SC.at[:, pl.ds(aligned(yy, 64), 64), :], sb_s.at[dy], sb_r.at[dy])

    @pl.loop(0, 8)
    def _(k):
        ST[:, pl.ds(aligned(k, BLK), BLK)] = SC[k].T

    def dot_chunk(i):
        lo, width = CHUNKS[i]
        tile = BLK if width % BLK == 0 else width

        for other in (True, False):
            blk = (1 - xl) if other else xl

            @pl.loop(0, width // tile)
            def _(t):
                cols = pl.ds(pl.multiple_of(lo + t * tile, HALF), tile)
                out = jnp.dot(
                    ST[pl.ds(aligned(blk, BLK), BLK), :], H[:, cols],
                    preferred_element_type=F32)
                if other:
                    RSS[:, cols] = out.astype(BF16)
                else:
                    ACC[:, cols] = out

            if other:
                cs = pl.ds(lo, width)
                send(RSS.at[:, cs], RSR.at[:, cs], rs_s.at[i], rs_r.at[i], dev(xl_=1 - xl))

    def wrow(zz, s, cc):
        return pl.ds(pl.multiple_of(((zz * 2 + s) * 2 + cc) * HALF, HALF), HALF)

    def adam_chunk(i):
        lo, width = CHUNKS[i]
        cs = pl.ds(lo, width)
        arrived(RSR.at[:, cs], rs_s.at[i], rs_r.at[i])
        for s in (0, 1):
            wbase = ((z * 2 + s) * 2 + c) * HALF

            @pl.loop(0, HALF // 16)
            def _(r):
                rows = pl.ds(pl.multiple_of(s * HALF + r * 16, 16), 16)
                wrows = pl.ds(pl.multiple_of(wbase + r * 16, 16), 16)
                grad = ACC[rows, cs] + RSR[rows, cs].astype(F32)
                new_moment = beta_one * MOM[rows, cs] + (1.0 - beta_one) * grad
                new_second = beta_two * SEC[rows, cs] + (1.0 - beta_two) * grad * grad
                update = new_moment / bias_one / (jnp.sqrt(new_second / bias_two) + adam_eps)
                new_master = MAS[rows, cs] - rate_learn * update
                MOM[rows, cs] = new_moment
                SEC[rows, cs] = new_second
                ACC[rows, cs] = update
                MAS[rows, cs] = new_master
                WB[wrows, cs] = new_master.astype(BF16)

    own_h.wait()
    h_forward_far(0)
    h_rest(0)
    dot_chunk(0)
    na_send(2)
    h_forward_near(1)
    h_forward_far(1)
    h_rest(1)
    dot_chunk(1)
    na_send(3)
    mas_cp.wait()
    mom_cp.wait()
    sec_cp.wait()
    h_forward_near(2)
    adam_chunk(0)
    h_forward_far(2)
    h_rest(2)
    dot_chunk(2)
    adam_chunk(1)
    adam_chunk(2)

    def w_view(zz, s, cc):
        return WB.at[wrow(zz, s, cc), :]

    for s in (0, 1):
        b = s * 7
        v = w_view(z, s, c)
        send(v, v, w_s.at[b], w_r.at[b], dev(z_=right))
        send(v, v, w_s.at[b + 1], w_r.at[b + 1], dev(z_=left))
        send(v, v, w_s.at[b + 2], w_r.at[b + 2], dev(c_=pc))
    outs = [
        local(MAS, mas_out), local(MOM, mom_out), local(SEC, sec_out), local(ACC, upd_out)]

    def w_wait(zz, s, cc, n):
        arrived(w_view(zz, s, cc), w_s.at[s * 7 + n], w_r.at[s * 7 + n])

    def w_send(zz, s, n, to):
        v = w_view(zz, s, c)
        send(v, v, w_s.at[s * 7 + n], w_r.at[s * 7 + n], to)

    def w_near(s):
        w_wait(left, s, c, 0)
        if s == 0:
            w_send(left, s, 5, dev(z_=right))
        w_send(left, s, 3, dev(c_=pc))
        w_wait(right, s, c, 1)
        if s == 1:
            w_send(right, s, 5, dev(z_=left))
        w_send(right, s, 4, dev(c_=pc))
        w_wait(left, s, pc, 3)
        w_wait(right, s, pc, 4)

    def w_far(s):
        w_wait(far, s, c, 5)
        w_send(far, s, 6, dev(c_=pc))
        w_wait(far, s, pc, 6)

    own_na.wait()

    def na_wait():
        for p in range(4):
            rows = pl.ds(p * HALF, HALF)
            arrived(NA.at[1 - xl, rows, :], na_s.at[p], na_r.at[p])

    conditional = []

    def project(e):
        dz, s = EVENTS[e]
        zz = mod4(z + dz)
        wcols = pl.ds(pl.multiple_of((zz * 2 + s) * BLK, BLK), BLK)
        slot = (dz // 2) * 2 + s
        mine = xl * 2 + xh
        same_xh = lax.rem(zz, 2) == xh

        @pl.loop(0, 4)
        def _(t):
            blk = t // 2
            rows = pl.ds(aligned(lax.rem(t, 2), BLK), BLK)
            out = lax.dot_general(
                NA[blk, rows, :], WB[wcols, :], (((1,), (1,)), ((), ())),
                preferred_element_type=F32)
            XS[e, blk, rows, :] = out.astype(BF16)

        for dx in (0, 1):
            blk = xl if dx == 0 else 1 - xl
            cp = remote(
                XS.at[e, blk], XB.at[slot, mine], x_s.at[e * 2 + dx], x_r.at[slot * 4 + mine],
                dev(xl_=blk, xh_=lax.rem(zz, 2)))
            if dx == 0:
                go = jnp.logical_not(same_xh)

                @pl.when(go)
                def _():
                    cp.start()

                @pl.when(same_xh)
                def _():
                    XB[slot, mine] = XS[e, blk]

                conditional.append((go, cp))
            else:
                cp.start()
                conditional.append((None, cp))

    def pair_sum(e):
        dz, s = EVENTS[e]
        zz = mod4(z + dz)
        slot = (dz // 2) * 2 + s
        for_me = lax.rem(zz, 2) == xh
        for h in (0, 1):
            yd = zz // 2 + 2 * h
            k = slot * 2 + h

            @pl.when(for_me)
            def _():
                for g in (0, 1):
                    src = h * 2 + g

                    @pl.when(src != xl * 2 + xh)
                    def _():
                        arrived(XB.at[slot, src], x_s.at[0], x_r.at[slot * 4 + src])

                @pl.loop(0, 4)
                def _(r):
                    rows = pl.ds(aligned(r, HALF), HALF)
                    YS[k, rows, :] = (
                        XB[slot, h * 2, rows, :].astype(F32)
                        + XB[slot, h * 2 + 1, rows, :].astype(F32)).astype(BF16)

            cp = remote(
                YS.at[k], YB.at[s, y], y_s.at[k], y_r.at[s * 4 + y], dev(y_=yd))
            go = jnp.logical_and(for_me, yd != y)
            stay = jnp.logical_and(for_me, yd == y)

            @pl.when(go)
            def _():
                cp.start()

            @pl.when(stay)
            def _():
                YB[s, y] = YS[k]

            return_later.append((go, cp))

    return_later = []

    w_wait(z, 0, pc, 2)
    na_wait()
    project(0)
    w_wait(z, 1, pc, 2)
    w_near(0)
    project(1)
    project(2)
    project(3)
    w_near(1)
    pair_sum(0)
    pair_sum(1)
    project(4)
    project(5)
    w_far(0)
    w_far(1)
    project(6)
    project(7)
    for e in range(2, 8):
        pair_sum(e)

    for s in (0, 1):
        for ys in range(4):
            @pl.when(ys != y)
            def _():
                arrived(YB.at[s, ys], y_s.at[0], y_r.at[s * 4 + ys])

        @pl.loop(0, 4)
        def _(r):
            rows = pl.ds(aligned(r, HALF), HALF)
            total = (YB[s, 0, rows, :].astype(F32) + YB[s, 1, rows, :].astype(F32)) + (
                YB[s, 2, rows, :].astype(F32) + YB[s, 3, rows, :].astype(F32))
            total = total.astype(BF16)
            NO[rows, s * HALF:(s + 1) * HALF] = total[:, :HALF]
            NO[rows, BLK + s * HALF:BLK + (s + 1) * HALF] = total[:, HALF:]

    outs.append(local(NO, next_out))
    for go, cp in sends + conditional + return_later:
        if go is None:
            cp.wait_send()
        else:
            @pl.when(go)
            def _():
                cp.wait_send()
    for cp in outs:
        cp.wait()


def body(out_grad, hidden_act, log_ratio, pair_order, seq_len, master, moment, second, next_act):
    block = jax.ShapeDtypeStruct((BLK, FL), F32)
    any_ = pl.BlockSpec(memory_space=pl.ANY)
    vm = pl.BlockSpec(memory_space=pltpu.VMEM)
    dma = pltpu.SemaphoreType.DMA
    return tuple(pl.pallas_call(
        kernel,
        name="fused_step",
        out_shape=(block, block, block, block, jax.ShapeDtypeStruct((512, 512), BF16)),
        in_specs=[any_, any_, vm, pl.BlockSpec(memory_space=pltpu.SMEM), vm, any_, any_, any_, any_],
        out_specs=[any_] * 5,
        scratch_shapes=[
            pltpu.VMEM((8 * BLK, FL), BF16),
            pltpu.VMEM((8, BLK, 512), BF16),
            pltpu.VMEM((512, 8 * BLK), BF16),
            pltpu.VMEM((8, 64, 512), BF16),
            pltpu.VMEM((64, 4096), BF16),
            pltpu.VMEM((BLK, FL), F32),
            pltpu.VMEM((BLK, FL), BF16),
            pltpu.VMEM((BLK, FL), BF16),
            pltpu.VMEM((BLK, FL), F32),
            pltpu.VMEM((BLK, FL), F32),
            pltpu.VMEM((BLK, FL), F32),
            pltpu.VMEM((8 * BLK, FL), BF16),
            pltpu.VMEM((2, 512, FL), BF16),
            pltpu.VMEM((8, 2, 512, BLK), BF16),
            pltpu.VMEM((4, 4, 512, BLK), BF16),
            pltpu.VMEM((8, 512, BLK), BF16),
            pltpu.VMEM((2, 4, 512, BLK), BF16),
            pltpu.VMEM((512, 512), BF16),
            dma((16,)),
            dma((27,)), dma((27,)), dma((8,)), dma((8,)), dma((4,)), dma((4,)),
            dma((3,)), dma((3,)), dma((4,)), dma((4,)), dma((14,)), dma((14,)),
            dma((16,)), dma((16,)), dma((8,)), dma((8,)),
        ],
        compiler_params=pltpu.CompilerParams(
            collective_id=0, has_side_effects=True, vmem_limit_bytes=62 << 20),
    )(out_grad, hidden_act, log_ratio.reshape(1, 8), pair_order, seq_len.reshape(1, 8),
      master, moment, second, next_act))


def solution(mesh):
    return jax.shard_map(
        body,
        mesh=mesh,
        in_specs=(
            P("dp", None), P("dp", "tensor"), P("dp"), P("dp", None), P("dp"),
            P("dp", "tensor"), P("dp", "tensor"), P("dp", "tensor"), P("dp", "tensor"),
        ),
        out_specs=(P("dp", "tensor"),) * 5,
        check_vma=False,
    )
```

time: 320 us -> 189 us (0.59)
  waiting for transfers between devices: 267 us -> 0 us
  Pallas kernels: 0 us -> 176 us
  matrix products: 25.7 us -> 0 us
  between operations: 13.8 us -> 0.66 us
  other arithmetic: 9.36 us -> 0 us
  local copies, waits for them, and re-layouts: 3.75 us -> 9.78 us
    reduce_scatter x2 -> x0, waiting for transfers between devices: 181 us -> none  [the longest x1 95.8 us: body(): lax.psum_scatter(lax.dot_general(scaled, hidden_act, (((0,), (0,)), ((),...]
    pallas_call x0 -> x1, Pallas kernels: none -> 176 us  [body(): pl.pallas_call(kernel, name='fused_step', out_shape=(block, block, block,...]
    all_gather x1 -> x0, waiting for transfers between devices: 85.7 us -> none  [body(): lax.all_gather(weights, 'dp', axis=0, tiled=True)]
    dot_general x2 -> x0, matrix products: 25.7 us -> none  [the longest x1 13.7 us: body(): lax.dot_general(next_act, lax.all_gather(weights, 'dp', axis=0, tiled=Tru...]
    unnamed x3 -> x13, local copies, waits for them, and re-layouts: 2.06 us -> 9.78 us
    convert_element_type x1 -> x0, other arithmetic: 7.65 us -> none  [body(): weights = new_master.astype(jnp.bfloat16)]
  transfers between devices with their start and end apart: 3 -> 0, of which waited for: 3 -> 0; matrix products, arithmetic and copies ran while one was open for 0% -> 0% of each run, Pallas kernels for 0% -> 0%
where the time goes in v1:
time: 189 us; the launch traced here: 186 us
  Pallas kernels  176 us (93%)
  local copies, waits for them, and re-layouts  9.78 us (5%)
    pallas_call x1, Pallas kernels, body(): pl.pallas_call(kernel, name='fused_step', out_shape=(block, block, block,...  176 us
    unnamed x13, local copies, waits for them, and re-layouts  9.78 us

profile of v1, /device:TPU:0, one launch (start us, length us, event | category | flops | bytes accessed | tf_op | source)
XLA Modules:
  0.0 186.5 jit_solution(7651735863688687964)
XLA Ops:
  0.6 176.0 %fused_step.1 = (f32[256,1920]{1,0:T(8,128)}, f32[256,1920]{1,0:T(8,128)}, f32[256,1920]{1,0:T(8,128)}, f32[256,1920]{1,0:T(8,128)}, bf16[512,512]{1,0:T(8,128)(2,1)}) custom-call(bf16[256,4096]{1,0:T(8,128)(2,1)} %og_hbm.1, bf16[256,1920]{1,0:T(8,128)(2,1)} %hid_hbm.1, f32[1,8]{1,0:T(1,128)} %bitcast.2, s32[1,8]{1,0:T(1,128)} %pair_ref.1, s32[1,8]{1,0:T(1,128)} %bitcast.3, ...), custom_call_target="tpu_custom_call" | custom-call | tf_op jit(solution)/shard_map/fused_step/pallas_call | solution.py:457
  176.7 0.0 copy-start.2
  176.7 3.1 %copy.19 = f32[256,1920]{1,0:T(8,128)} copy(f32[256,1920]{1,0:T(8,128)} %get-tuple-element.10) | data formatting | bytes 3932160
  179.8 0.0 copy-done.2
  179.8 0.0 copy-start.1
  179.8 1.3 copy.20
  181.0 1.0 copy-done.1
  182.0 0.0 copy-start
  182.0 1.3 copy.21
  183.3 1.0 copy-done
  184.3 0.0 copy-start.3
  184.3 1.3 copy.22
  185.6 0.1 copy-done.3
  185.7 0.8 copy.23
Async XLA Ops:
  176.7 3.1 %copy-start.2 = (f32[256,1920]{1,0:T(8,128)S(1)}, f32[256,1920]{1,0:T(8,128)}, u32[]{:S(2)}) copy-start(f32[256,1920]{1,0:T(8,128)} %get-tuple-element.11) | copy-start | bytes 5898244
  179.8 2.3 %copy-start.1 = (f32[256,1920]{1,0:T(8,128)S(1)}, f32[256,1920]{1,0:T(8,128)}, u32[]{:S(2)}) copy-start(f32[256,1920]{1,0:T(8,128)} %get-tuple-element.12) | copy-start | bytes 5898244
  182.0 2.3 %copy-start = (f32[256,1920]{1,0:T(8,128)S(1)}, f32[256,1920]{1,0:T(8,128)}, u32[]{:S(2)}) copy-start(f32[256,1920]{1,0:T(8,128)} %get-tuple-element.13) | copy-start | bytes 5898244
  184.3 1.4 copy-start.3

commit v2 on v1

v2 whole, which is shorter than its diff:
```python
import jax
import jax.numpy as jnp
from jax import lax
from jax.experimental import pallas as pl
from jax.experimental.pallas import tpu as pltpu
from jax.sharding import PartitionSpec as P

LEN = 32
beta_dpo = 0.1
beta_one = 0.9
beta_two = 0.999
bias_one = 1.0 - 0.9**10
bias_two = 1.0 - 0.999**10
adam_eps = 1e-08
rate_learn = 0.001

MESH = pl.DeviceIdType.MESH
F32 = jnp.float32
BF16 = jnp.bfloat16

FL = 1920
BLK = 256
HALF = 128
CHUNKS = ((0, 384), (384, 512), (896, 512), (1408, 384), (1792, 128))
UNIT = 64


def mod4(v):
    return lax.rem(v + 8, 4)


def kernel(
    og_hbm, hid_hbm, ratio_ref, pair_ref, len_ref, mas_hbm, mom_hbm, sec_hbm, nact_hbm,
    MAS, MOM, SEC, ACC, NO,
    H, SC, ST, SS, OG, RSS, RSR, WB, NA, XS, XB, YS, YB, YF,
    loc_sem,
    ha_s, ha_r, sa_s, sa_r, sb_s, sb_r, rs_s, rs_r, na_s, na_r, w_s, w_r, x_s, x_r, y_s, y_r, f_s, f_r,
):
    dp = lax.axis_index("dp")
    tn = lax.axis_index("tensor")
    xl = dp // 8
    z = lax.rem(dp // 2, 4)
    c = lax.rem(dp, 2)
    y = tn // 2
    xh = lax.rem(tn, 2)

    def dev(xl_=None, z_=None, c_=None, y_=None, xh_=None):
        xl_ = xl if xl_ is None else xl_
        z_ = z if z_ is None else z_
        c_ = c if c_ is None else c_
        y_ = y if y_ is None else y_
        xh_ = xh if xh_ is None else xh_
        return (xl_ * 8 + z_ * 2 + c_, y_ * 2 + xh_)

    right, left, far = mod4(z + 1), mod4(z - 1), mod4(z + 2)
    pc = 1 - c

    barrier = pltpu.get_barrier_semaphore()
    for k in range(1, 16):
        idx = lax.rem(xl * 8 + tn + k, 16)
        pl.semaphore_signal(
            barrier, inc=1,
            device_id=((idx // 8) * 8 + z * 2 + c, lax.rem(idx, 8)), device_id_type=MESH)
    for k in range(1, 8):
        idx = lax.rem(z * 2 + c + k, 8)
        pl.semaphore_signal(
            barrier, inc=1, device_id=(xl * 8 + idx, tn), device_id_type=MESH)

    locals_ = []

    def local(src, dst):
        cp = pltpu.make_async_copy(src, dst, loc_sem.at[len(locals_)])
        cp.start()
        locals_.append(cp)
        return cp

    def aligned(v, m):
        return pl.multiple_of(v * m, m)

    qrows = pl.ds(aligned(y, 64), 64)
    og_cp = local(og_hbm.at[qrows, :], OG)
    own_h = local(hid_hbm, H.at[pl.ds(aligned(z * 2 + c, BLK), BLK), :])
    mas_cp = local(mas_hbm, MAS)
    mom_cp = local(mom_hbm, MOM)
    sec_cp = local(sec_hbm, SEC)
    own_na = local(nact_hbm, NA.at[xl])
    sends = []

    def remote(src, dst, ss, rs, to):
        return pltpu.make_async_remote_copy(
            src, dst, ss, rs, device_id=to, device_id_type=MESH)

    def send(src, dst, ss, rs, to):
        cp = remote(src, dst, ss, rs, to)
        cp.start()
        sends.append((None, cp))

    def arrived(dst, ss, rs):
        remote(dst, dst, ss, rs, (dp, tn)).wait_recv()

    def hrow(zz, cc, half=None):
        if half is None:
            return pl.ds(aligned(zz * 2 + cc, BLK), BLK)
        return pl.ds(pl.multiple_of((zz * 2 + cc) * BLK + half * HALF, HALF), HALF)

    def h_own(i):
        cs = pl.ds(CHUNKS[i][0], CHUNKS[i][1])
        src = hid_hbm.at[:, cs]
        dst = H.at[hrow(z, c), cs]
        b = i * 9
        send(src, dst, ha_s.at[b], ha_r.at[b], dev(z_=right))
        send(src, dst, ha_s.at[b + 1], ha_r.at[b + 1], dev(z_=left))
        send(src, dst, ha_s.at[b + 2], ha_r.at[b + 2], dev(c_=pc))

    def h_view(i, zz, cc, half=None):
        return H.at[hrow(zz, cc, half), pl.ds(CHUNKS[i][0], CHUNKS[i][1])]

    def h_forward_near(i):
        b = i * 9
        v = h_view(i, left, c)
        arrived(v, ha_s.at[b], ha_r.at[b])
        v0 = h_view(i, left, c, 0)
        send(v0, v0, ha_s.at[b + 5], ha_r.at[b + 5], dev(z_=right))
        send(v, v, ha_s.at[b + 3], ha_r.at[b + 3], dev(c_=pc))
        v = h_view(i, right, c)
        arrived(v, ha_s.at[b + 1], ha_r.at[b + 1])
        v1 = h_view(i, right, c, 1)
        send(v1, v1, ha_s.at[b + 6], ha_r.at[b + 6], dev(z_=left))
        send(v, v, ha_s.at[b + 4], ha_r.at[b + 4], dev(c_=pc))

    def h_forward_far(i):
        b = i * 9
        for half in (0, 1):
            v = h_view(i, far, c, half)
            arrived(v, ha_s.at[b + 5 + half], ha_r.at[b + 5 + half])
            send(v, v, ha_s.at[b + 7 + half], ha_r.at[b + 7 + half], dev(c_=pc))

    def h_rest(i):
        b = i * 9
        arrived(h_view(i, z, pc), ha_s.at[b + 2], ha_r.at[b + 2])
        arrived(h_view(i, left, pc), ha_s.at[b + 3], ha_r.at[b + 3])
        arrived(h_view(i, right, pc), ha_s.at[b + 4], ha_r.at[b + 4])
        for half in (0, 1):
            arrived(h_view(i, far, pc, half), ha_s.at[b + 7 + half], ha_r.at[b + 7 + half])

    def na_send(p):
        rows = pl.ds(p * HALF, HALF)
        send(nact_hbm.at[rows, :], NA.at[xl, rows, :], na_s.at[p], na_r.at[p], dev(xl_=1 - xl))

    lane = lax.broadcasted_iota(jnp.int32, (1, 8), 1)
    ratios = ratio_ref[...]
    coef = jnp.zeros((1, 8), F32)
    for p in range(4):
        oc = (lane == pair_ref[0, 2 * p]).astype(F32)
        orj = (lane == pair_ref[0, 2 * p + 1]).astype(F32)
        margin = beta_dpo * (
            jnp.sum(oc * ratios, axis=1, keepdims=True)
            - jnp.sum(orj * ratios, axis=1, keepdims=True))
        weight = beta_dpo * jax.nn.sigmoid(-margin)
        coef = coef + weight * (orj - oc)
    row = lax.broadcasted_iota(jnp.int32, (64, 8), 0)
    lane64 = lax.broadcasted_iota(jnp.int32, (64, 8), 1)
    upper = (row >= LEN).astype(jnp.int32)
    sel = (lane64 == 2 * y + upper).astype(F32)
    row_coef = jnp.sum(sel * coef, axis=1, keepdims=True)
    row_len = jnp.sum(sel * len_ref[...].astype(F32), axis=1, keepdims=True)
    pos = (row - LEN * upper)[:, 0:1].astype(F32)
    factor = row_coef * (pos < row_len).astype(F32)
    og_cp.wait()

    def scale(b):
        xlb = (1 - xl) if b == 0 else xl
        for dz in range(4):
            for dc in range(2):
                zz = mod4(z + dz)
                cc = c if dc == 0 else pc
                k = dz * 2 + dc
                cols = pl.ds(aligned(xlb * 8 + zz * 2 + cc, BLK), BLK)
                rows = (OG[:, cols].astype(F32) * factor).astype(BF16)
                if k == 0:
                    SC[b, z * 2 + c, qrows, :] = rows
                else:
                    SS[b, k] = rows

    def scale_send(b):
        for dz in range(4):
            for dc in range(2):
                zz = mod4(z + dz)
                cc = c if dc == 0 else pc
                k = dz * 2 + dc
                if k:
                    send(SS.at[b, k], SC.at[b, z * 2 + c, qrows, :],
                         sa_s.at[b * 8 + k], sa_r.at[b * 8 + k], dev(z_=zz, c_=cc))

    def share_rows(b):
        for dz in range(4):
            for dc in range(2):
                k = dz * 2 + dc
                if k:
                    zz = mod4(z - dz)
                    cc = c if dc == 0 else pc
                    arrived(SC.at[b, zz * 2 + cc, qrows, :], sa_s.at[b * 8 + k], sa_r.at[b * 8 + k])
        for dy in (1, 3, 2):
            v = SC.at[b, :, qrows, :]
            send(v, v, sb_s.at[b * 4 + dy], sb_r.at[b * 4 + dy], dev(y_=mod4(y + dy)))

    def turn(b):
        for dy in (1, 3, 2):
            yy = mod4(y - dy)
            arrived(SC.at[b, :, pl.ds(aligned(yy, 64), 64), :],
                    sb_s.at[b * 4 + dy], sb_r.at[b * 4 + dy])

        @pl.loop(0, 8)
        def _(k):
            ST[b, :, pl.ds(aligned(k, BLK), BLK)] = SC[b, k].T

    def dot_chunk(i, b):
        cs = pl.ds(CHUNKS[i][0], CHUNKS[i][1])
        out = jnp.dot(ST[b], H[:, cs], preferred_element_type=F32)
        if b == 0:
            RSS[:, cs] = out.astype(BF16)
            send(RSS.at[:, cs], RSR.at[:, cs], rs_s.at[i], rs_r.at[i], dev(xl_=1 - xl))
        else:
            ACC[:, cs] = out

    def adam_chunk(i):
        lo, width = CHUNKS[i]
        cs = pl.ds(lo, width)
        arrived(RSR.at[:, cs], rs_s.at[i], rs_r.at[i])
        for s in (0, 1):
            wbase = ((z * 2 + s) * 2 + c) * HALF

            @pl.loop(0, HALF // 16)
            def _(r):
                rows = pl.ds(pl.multiple_of(s * HALF + r * 16, 16), 16)
                wrows = pl.ds(pl.multiple_of(wbase + r * 16, 16), 16)
                grad = ACC[rows, cs] + RSR[rows, cs].astype(F32)
                new_moment = beta_one * MOM[rows, cs] + (1.0 - beta_one) * grad
                new_second = beta_two * SEC[rows, cs] + (1.0 - beta_two) * grad * grad
                update = new_moment / bias_one / (jnp.sqrt(new_second / bias_two) + adam_eps)
                new_master = MAS[rows, cs] - rate_learn * update
                MOM[rows, cs] = new_moment
                SEC[rows, cs] = new_second
                ACC[rows, cs] = update
                MAS[rows, cs] = new_master
                WB[wrows, cs] = new_master.astype(BF16)

    scale(0)
    scale(1)
    pl.semaphore_wait(barrier, 22)
    scale_send(0)
    h_own(0)
    na_send(0)
    na_send(1)
    scale_send(1)
    h_own(1)
    share_rows(0)
    h_forward_near(0)
    h_own(2)
    share_rows(1)
    h_forward_near(1)
    h_own(3)
    h_forward_far(0)
    own_h.wait()
    turn(0)
    h_rest(0)
    dot_chunk(0, 0)
    h_forward_near(2)
    h_own(4)
    h_forward_far(1)
    h_rest(1)
    dot_chunk(1, 0)
    h_forward_near(3)
    h_forward_far(2)
    h_rest(2)
    dot_chunk(2, 0)
    turn(1)
    dot_chunk(0, 1)
    h_forward_near(4)
    h_forward_far(3)
    h_rest(3)
    dot_chunk(3, 0)
    mas_cp.wait()
    mom_cp.wait()
    sec_cp.wait()
    adam_chunk(0)
    dot_chunk(1, 1)
    adam_chunk(1)
    dot_chunk(2, 1)
    h_forward_far(4)
    h_rest(4)
    dot_chunk(4, 0)
    na_send(2)
    na_send(3)
    adam_chunk(2)
    dot_chunk(3, 1)
    dot_chunk(4, 1)
    adam_chunk(3)
    adam_chunk(4)

    def w_view(zz, u, cc):
        row = ((zz * 2 + u // 2) * 2 + cc) * HALF + (u % 2) * UNIT
        return WB.at[pl.ds(pl.multiple_of(row, UNIT), UNIT), :]

    def w_send(zz, u, n, to):
        v = w_view(zz, u, c)
        send(v, v, w_s.at[u * 7 + n], w_r.at[u * 7 + n], to)

    def w_wait(zz, u, cc, n):
        arrived(w_view(zz, u, cc), w_s.at[u * 7 + n], w_r.at[u * 7 + n])

    def w_own(u):
        w_send(z, u, 0, dev(z_=right))
        w_send(z, u, 1, dev(z_=left))

    def w_near(u):
        w_wait(left, u, c, 0)
        if u % 2 == 0:
            w_send(left, u, 5, dev(z_=right))
        w_send(left, u, 3, dev(c_=pc))
        w_wait(right, u, c, 1)
        if u % 2 == 1:
            w_send(right, u, 5, dev(z_=left))
        w_send(right, u, 4, dev(c_=pc))

    def w_near_rest(u):
        w_wait(left, u, pc, 3)
        w_wait(right, u, pc, 4)

    def w_far(u):
        w_wait(far, u, c, 5)
        w_send(far, u, 6, dev(c_=pc))

    for u in range(4):
        w_send(z, u, 2, dev(c_=pc))
        if u < 3:
            w_own(u)
    own_na.wait()

    def na_wait():
        for p in range(4):
            rows = pl.ds(p * HALF, HALF)
            arrived(NA.at[1 - xl, rows, :], na_s.at[p], na_r.at[p])

    conditional = []

    zzs = (z, 3 - z, mod4(5 - z), far)
    role = mod4(y - 2 * xl)

    def multiply(kind, s, side):
        wcols = pl.ds(aligned(zzs[kind] * 2 + s, BLK), BLK)
        e = kind * 2 + s
        blk = xl if side == 0 else 1 - xl

        @pl.loop(0, 2)
        def _(t):
            rows = pl.ds(aligned(t, BLK), BLK)
            out = lax.dot_general(
                NA[blk, rows, :], WB[wcols, :], (((1,), (1,)), ((), ())),
                preferred_element_type=F32)
            XS[e, side, rows, :] = out.astype(BF16)

    def start_if(go, cp):
        @pl.when(go)
        def _():
            cp.start()

        conditional.append((go, cp))

    def y_start(kind, s, side):
        multiply(kind, s, side)
        e = kind * 2 + s
        n = e * 2 + side
        h = zzs[kind] // 2
        src = XS.at[e, side]
        start_if(role == 2 + h, remote(
            src, YF.at[n, 0], f_s.at[n], f_r.at[2 * n], dev(y_=mod4(2 * xl + 3 - h))))
        start_if(role == 1 - h, remote(
            src, YF.at[n, 1], f_s.at[n], f_r.at[2 * n + 1], dev(y_=2 * xl + h)))

    def y_middle(kind, s, side):
        e = kind * 2 + s
        n = e * 2 + side
        h = zzs[kind] // 2
        go = role == 3 - h

        @pl.when(go)
        def _():
            arrived(YF.at[n, 0], f_s.at[n], f_r.at[2 * n])

            @pl.loop(0, 4)
            def _(r):
                rows = pl.ds(aligned(r, HALF), HALF)
                XS[e, side, rows, :] = (
                    XS[e, side, rows, :].astype(F32) + YF[n, 0, rows, :].astype(F32)).astype(BF16)

        start_if(go, remote(
            XS.at[e, side], YF.at[n, 0], f_s.at[n], f_r.at[2 * n], dev(y_=2 * xl + h)))

    def y_end(kind, s, side):
        e = kind * 2 + s
        n = e * 2 + side
        zz = zzs[kind]
        h = zz // 2
        last = role == h
        blk = xl if side == 0 else 1 - xl

        @pl.when(last)
        def _():
            for g in (0, 1):
                arrived(YF.at[n, g], f_s.at[n], f_r.at[2 * n + g])

            @pl.loop(0, 4)
            def _(r):
                rows = pl.ds(aligned(r, HALF), HALF)
                XS[e, side, rows, :] = (
                    (XS[e, side, rows, :].astype(F32) + YF[n, 1, rows, :].astype(F32))
                    + YF[n, 0, rows, :].astype(F32)).astype(BF16)

        cp = remote(XS.at[e, side], YB.at[s, xh], f_s.at[n], y_r.at[s * 4 + xh],
                    dev(xl_=blk, xh_=lax.rem(zz, 2)))
        if side == 0:
            same = lax.rem(zz, 2) == xh
            start_if(jnp.logical_and(last, jnp.logical_not(same)), cp)

            @pl.when(jnp.logical_and(last, same))
            def _():
                YB[s, xh] = XS[e, side]
        else:
            start_if(last, cp)

    def x_start(kind, s, side):
        multiply(kind, s, side)
        e = kind * 2 + s
        zz = zzs[kind]
        mine = xl * 2 + xh
        blk = xl if side == 0 else 1 - xl
        cp = remote(
            XS.at[e, side], XB.at[s, mine], x_s.at[(e - 4) * 2 + side], x_r.at[s * 4 + mine],
            dev(xl_=blk, xh_=lax.rem(zz, 2)))
        if side == 0:
            stay = lax.rem(zz, 2) == xh
            start_if(jnp.logical_not(stay), cp)

            @pl.when(stay)
            def _():
                XB[s, mine] = XS[e, side]
        else:
            cp.start()
            conditional.append((None, cp))

    def pair_sum(kind, s, side):
        zz = zzs[kind]
        for_me = lax.rem(zz, 2) == xh
        h = xl if side == 0 else 1 - xl
        yd = zz // 2 + 2 * h
        k = s * 2 + side

        @pl.when(for_me)
        def _():
            for g in (0, 1):
                src = h * 2 + g
                if side == 0:
                    @pl.when(g != xh)
                    def _():
                        arrived(XB.at[s, src], x_s.at[0], x_r.at[s * 4 + src])
                else:
                    arrived(XB.at[s, src], x_s.at[0], x_r.at[s * 4 + src])

            @pl.loop(0, 4)
            def _(r):
                rows = pl.ds(aligned(r, HALF), HALF)
                YS[k, rows, :] = (
                    XB[s, h * 2, rows, :].astype(F32)
                    + XB[s, h * 2 + 1, rows, :].astype(F32)).astype(BF16)

        start_if(jnp.logical_and(for_me, yd != y), remote(
            YS.at[k], YB.at[s, y], y_s.at[k], y_r.at[s * 4 + y], dev(y_=yd)))

        @pl.when(jnp.logical_and(for_me, yd == y))
        def _():
            YB[s, y] = YS[k]

    for u in range(4):
        w_wait(z, u, pc, 2)
    y_start(0, 0, 0)
    y_start(0, 1, 0)
    w_near(0)
    w_near(1)
    w_own(3)
    w_near_rest(0)
    w_near_rest(1)
    y_start(1, 0, 0)
    x_start(2, 0, 0)
    y_middle(0, 0, 0)
    y_middle(0, 1, 0)
    w_near(2)
    w_far(0)
    w_far(1)
    na_wait()
    x_start(2, 0, 1)
    y_start(0, 0, 1)
    y_start(0, 1, 1)
    y_start(1, 0, 1)
    w_wait(far, 0, pc, 6)
    w_wait(far, 1, pc, 6)
    x_start(3, 0, 0)
    x_start(3, 0, 1)
    y_middle(1, 0, 0)
    y_end(0, 0, 0)
    y_end(0, 1, 0)
    w_near(3)
    w_near_rest(2)
    w_near_rest(3)
    for side in (0, 1):
        x_start(2, 1, side)
        y_start(1, 1, side)
    y_middle(0, 0, 1)
    y_middle(0, 1, 1)
    y_middle(1, 0, 1)
    pair_sum(2, 0, 0)
    pair_sum(2, 0, 1)
    w_far(2)
    w_far(3)
    w_wait(far, 2, pc, 6)
    w_wait(far, 3, pc, 6)
    x_start(3, 1, 0)
    x_start(3, 1, 1)
    y_end(1, 0, 0)
    y_end(0, 0, 1)
    y_end(0, 1, 1)
    y_end(1, 0, 1)
    y_middle(1, 1, 0)
    y_middle(1, 1, 1)
    pair_sum(3, 0, 0)
    pair_sum(3, 0, 1)
    pair_sum(2, 1, 0)
    pair_sum(2, 1, 1)
    y_end(1, 1, 0)
    y_end(1, 1, 1)
    pair_sum(3, 1, 0)
    pair_sum(3, 1, 1)

    zd = lax.rem(y, 2) * 2 + xh
    by_y = jnp.logical_or(zd == z, zd == 3 - z)
    by_x = jnp.logical_not(by_y)

    def finish(s, count):
        @pl.loop(0, 4)
        def _(r):
            rows = pl.ds(aligned(r, HALF), HALF)
            total = YB[s, 0, rows, :].astype(F32) + YB[s, 1, rows, :].astype(F32)
            if count == 4:
                total = total + (YB[s, 2, rows, :].astype(F32) + YB[s, 3, rows, :].astype(F32))
            total = total.astype(BF16)
            NO[rows, s * HALF:(s + 1) * HALF] = total[:, :HALF]
            NO[rows, BLK + s * HALF:BLK + (s + 1) * HALF] = total[:, HALF:]

    for s in (0, 1):
        for g in (0, 1):
            away = jnp.logical_or(y // 2 != xl, g != xh)

            @pl.when(jnp.logical_and(by_y, away))
            def _():
                arrived(YB.at[s, g], y_s.at[0], y_r.at[s * 4 + g])

        for ys in range(4):
            @pl.when(jnp.logical_and(by_x, ys != y))
            def _():
                arrived(YB.at[s, ys], y_s.at[0], y_r.at[s * 4 + ys])

        @pl.when(by_y)
        def _():
            finish(s, 2)

        @pl.when(by_x)
        def _():
            finish(s, 4)

    for go, cp in sends + conditional:
        if go is None:
            cp.wait_send()
        else:
            @pl.when(go)
            def _():
                cp.wait_send()


def body(out_grad, hidden_act, log_ratio, pair_order, seq_len, master, moment, second, next_act):
    block = jax.ShapeDtypeStruct((BLK, FL), F32)
    any_ = pl.BlockSpec(memory_space=pl.ANY)
    vm = pl.BlockSpec(memory_space=pltpu.VMEM)
    dma = pltpu.SemaphoreType.DMA
    results = (block, block, block, block, jax.ShapeDtypeStruct((512, 512), BF16))
    return tuple(pl.pallas_call(
        kernel,
        name="fused_step",
        out_shape=tuple(pltpu.VMEM(r.shape, r.dtype) for r in results),
        in_specs=[any_, any_, vm, pl.BlockSpec(memory_space=pltpu.SMEM), vm, any_, any_, any_, any_],
        out_specs=[vm] * 5,
        scratch_shapes=[
            pltpu.VMEM((8 * BLK, FL), BF16),
            pltpu.VMEM((2, 8, BLK, BLK), BF16),
            pltpu.VMEM((2, BLK, 8 * BLK), BF16),
            pltpu.VMEM((2, 8, 64, BLK), BF16),
            pltpu.VMEM((64, 4096), BF16),
            pltpu.VMEM((BLK, FL), BF16),
            pltpu.VMEM((BLK, FL), BF16),
            pltpu.VMEM((8 * BLK, FL), BF16),
            pltpu.VMEM((2, 512, FL), BF16),
            pltpu.VMEM((8, 2, 512, BLK), BF16),
            pltpu.VMEM((2, 4, 512, BLK), BF16),
            pltpu.VMEM((4, 512, BLK), BF16),
            pltpu.VMEM((2, 4, 512, BLK), BF16),
            pltpu.VMEM((8, 2, 512, BLK), BF16),
            dma((16,)),
            dma((45,)), dma((45,)), dma((16,)), dma((16,)), dma((8,)), dma((8,)),
            dma((5,)), dma((5,)), dma((4,)), dma((4,)), dma((28,)), dma((28,)),
            dma((8,)), dma((8,)), dma((4,)), dma((8,)), dma((8,)), dma((16,)),
        ],
        compiler_params=pltpu.CompilerParams(
            collective_id=0, has_side_effects=True, vmem_limit_bytes=52 << 20),
    )(out_grad, hidden_act, log_ratio.reshape(1, 8), pair_order, seq_len.reshape(1, 8),
      master, moment, second, next_act))


def solution(mesh):
    return jax.shard_map(
        body,
        mesh=mesh,
        in_specs=(
            P("dp", None), P("dp", "tensor"), P("dp"), P("dp", None), P("dp"),
            P("dp", "tensor"), P("dp", "tensor"), P("dp", "tensor"), P("dp", "tensor"),
        ),
        out_specs=(P("dp", "tensor"),) * 5,
        check_vma=False,
    )
```

time: 189 us -> 145 us (0.77)
  Pallas kernels: 176 us -> 137 us
  local copies, waits for them, and re-layouts: 9.78 us -> 5.88 us
    pallas_call x1, Pallas kernels: 176 us -> 137 us  [body(): pl.pallas_call(kernel, name='fused_step', out_shape=tuple((pltpu.VMEM(r.s...]
    unnamed x13 -> x5, local copies, waits for them, and re-layouts: 9.78 us -> 5.88 us
where the time goes in v2:
time: 145 us; the launch traced here: 144 us
  Pallas kernels  137 us (94%)
  local copies, waits for them, and re-layouts  5.88 us (4%)
    pallas_call x1, Pallas kernels, body(): pl.pallas_call(kernel, name='fused_step', out_shape=tuple((pltpu.VMEM(r.s...  137 us
    unnamed x5, local copies, waits for them, and re-layouts  5.88 us

profile of v2, /device:TPU:0, one launch (start us, length us, event | category | flops | bytes accessed | tf_op | source)
XLA Modules:
  0.0 143.5 jit_solution(8785020600485382526)
XLA Ops:
  0.6 137.0 %fused_step.1 = (f32[256,1920]{1,0:T(8,128)S(1)}, f32[256,1920]{1,0:T(8,128)S(1)}, f32[256,1920]{1,0:T(8,128)S(1)}, f32[256,1920]{1,0:T(8,128)S(1)}, bf16[512,512]{1,0:T(8,128)(2,1)S(1)}) custom-call(bf16[256,4096]{1,0:T(8,128)(2,1)} %og_hbm.1, bf16[256,1920]{1,0:T(8,128)(2,1)} %hid_hbm.1, f32[1,8]{1,0:T(1,128)} %bitcast.2, s32[1,8]{1,0:T(1,128)} %pair_ref.1, ...), custom_call_target="tpu_custom_call" | custom-call | tf_op jit(solution)/shard_map/fused_step/pallas_call | solution.py:595
  137.6 1.3 copy.19
  138.9 0.8 copy.23
  139.7 1.3 copy.20
  141.0 1.3 copy.21
  142.2 1.3 copy.22

commit v3 on v2

--- a/solution.py
+++ b/solution.py
@@ -244,6 +244,52 @@
                 ACC[rows, cs] = update
                 MAS[rows, cs] = new_master
                 WB[wrows, cs] = new_master.astype(BF16)
+
+    def w_view(zz, u, cc):
+        row = ((zz * 2 + u // 2) * 2 + cc) * HALF + (u % 2) * UNIT
+        return WB.at[pl.ds(pl.multiple_of(row, UNIT), UNIT), :]
+
+    def w_send(zz, u, n, to):
+        v = w_view(zz, u, c)
+        send(v, v, w_s.at[u * 9 + n], w_r.at[u * 9 + n], to)
+
+    def w_wait(zz, u, cc, n):
+        arrived(w_view(zz, u, cc), w_s.at[u * 9 + n], w_r.at[u * 9 + n])
+
+    def w_part(zz, u, part):
+        cols = pl.ds(0, 1408) if part == 0 else pl.ds(1408, 512)
+        row = ((zz * 2 + u // 2) * 2 + c) * HALF + (u % 2) * UNIT
+        return WB.at[pl.ds(pl.multiple_of(row, UNIT), UNIT), cols]
+
+    def w_own(part):
+        for u in range(4):
+            v = w_part(z, u, part)
+            for n, to in ((0, right), (1, left)):
+                k = u * 9 + n + 7 * part
+                send(v, v, w_s.at[k], w_r.at[k], dev(z_=to))
+
+    def w_arrived(zz, u, n):
+        for part in (0, 1):
+            k = u * 9 + n + 7 * part
+            arrived(w_part(zz, u, part), w_s.at[k], w_r.at[k])
+
+    def w_near(u):
+        w_arrived(left, u, 0)
+        if u % 2 == 0:
+            w_send(left, u, 5, dev(z_=right))
+        w_send(left, u, 3, dev(c_=pc))
+        w_arrived(right, u, 1)
+        if u % 2 == 1:
+            w_send(right, u, 5, dev(z_=left))
+        w_send(right, u, 4, dev(c_=pc))
+
+    def w_near_rest(u):
+        w_wait(left, u, pc, 3)
+        w_wait(right, u, pc, 4)
+
+    def w_far(u):
+        w_wait(far, u, c, 5)
+        w_send(far, u, 6, dev(c_=pc))
 
     scale(0)
     scale(1)
@@ -287,54 +333,21 @@
     dot_chunk(1, 1)
     adam_chunk(1)
     dot_chunk(2, 1)
+    adam_chunk(2)
+    w_own(0)
     h_forward_far(4)
     h_rest(4)
     dot_chunk(4, 0)
     na_send(2)
     na_send(3)
-    adam_chunk(2)
     dot_chunk(3, 1)
     dot_chunk(4, 1)
     adam_chunk(3)
     adam_chunk(4)
 
-    def w_view(zz, u, cc):
-        row = ((zz * 2 + u // 2) * 2 + cc) * HALF + (u % 2) * UNIT
-        return WB.at[pl.ds(pl.multiple_of(row, UNIT), UNIT), :]
-
-    def w_send(zz, u, n, to):
-        v = w_view(zz, u, c)
-        send(v, v, w_s.at[u * 7 + n], w_r.at[u * 7 + n], to)
-
-    def w_wait(zz, u, cc, n):
-        arrived(w_view(zz, u, cc), w_s.at[u * 7 + n], w_r.at[u * 7 + n])
-
-    def w_own(u):
-        w_send(z, u, 0, dev(z_=right))
-        w_send(z, u, 1, dev(z_=left))
-
-    def w_near(u):
-        w_wait(left, u, c, 0)
-        if u % 2 == 0:
-            w_send(left, u, 5, dev(z_=right))
-        w_send(left, u, 3, dev(c_=pc))
-        w_wait(right, u, c, 1)
-        if u % 2 == 1:
-            w_send(right, u, 5, dev(z_=left))
-        w_send(right, u, 4, dev(c_=pc))
-
-    def w_near_rest(u):
-        w_wait(left, u, pc, 3)
-        w_wait(right, u, pc, 4)
-
-    def w_far(u):
-        w_wait(far, u, c, 5)
-        w_send(far, u, 6, dev(c_=pc))
-
+    w_own(1)
     for u in range(4):
         w_send(z, u, 2, dev(c_=pc))
-        if u < 3:
-            w_own(u)
     own_na.wait()
 
     def na_wait():
@@ -487,34 +500,34 @@
     y_start(0, 1, 0)
     w_near(0)
     w_near(1)
-    w_own(3)
     w_near_rest(0)
     w_near_rest(1)
     y_start(1, 0, 0)
     x_start(2, 0, 0)
+    w_near(2)
+    w_near(3)
     y_middle(0, 0, 0)
     y_middle(0, 1, 0)
-    w_near(2)
-    w_far(0)
-    w_far(1)
     na_wait()
     x_start(2, 0, 1)
     y_start(0, 0, 1)
     y_start(0, 1, 1)
     y_start(1, 0, 1)
+    w_far(0)
+    w_far(1)
+    w_near_rest(2)
+    w_near_rest(3)
+    y_middle(1, 0, 0)
+    y_end(0, 0, 0)
+    y_end(0, 1, 0)
+    x_start(2, 1, 0)
+    y_start(1, 1, 0)
     w_wait(far, 0, pc, 6)
     w_wait(far, 1, pc, 6)
     x_start(3, 0, 0)
     x_start(3, 0, 1)
-    y_middle(1, 0, 0)
-    y_end(0, 0, 0)
-    y_end(0, 1, 0)
-    w_near(3)
-    w_near_rest(2)
-    w_near_rest(3)
-    for side in (0, 1):
-        x_start(2, 1, side)
-        y_start(1, 1, side)
+    x_start(2, 1, 1)
+    y_start(1, 1, 1)
     y_middle(0, 0, 1)
     y_middle(0, 1, 1)
     y_middle(1, 0, 1)
@@ -526,20 +539,20 @@
     w_wait(far, 3, pc, 6)
     x_start(3, 1, 0)
     x_start(3, 1, 1)
+    pair_sum(3, 0, 0)
+    pair_sum(3, 0, 1)
+    y_middle(1, 1, 0)
     y_end(1, 0, 0)
+    pair_sum(2, 1, 0)
+    y_middle(1, 1, 1)
     y_end(0, 0, 1)
+    pair_sum(2, 1, 1)
     y_end(0, 1, 1)
     y_end(1, 0, 1)
-    y_middle(1, 1, 0)
-    y_middle(1, 1, 1)
-    pair_sum(3, 0, 0)
-    pair_sum(3, 0, 1)
-    pair_sum(2, 1, 0)
-    pair_sum(2, 1, 1)
+    pair_sum(3, 1, 0)
+    pair_sum(3, 1, 1)
     y_end(1, 1, 0)
     y_end(1, 1, 1)
-    pair_sum(3, 1, 0)
-    pair_sum(3, 1, 1)
 
     zd = lax.rem(y, 2) * 2 + xh
     by_y = jnp.logical_or(zd == z, zd == 3 - z)
@@ -615,7 +628,7 @@
             pltpu.VMEM((8, 2, 512, BLK), BF16),
             dma((16,)),
             dma((45,)), dma((45,)), dma((16,)), dma((16,)), dma((8,)), dma((8,)),
-            dma((5,)), dma((5,)), dma((4,)), dma((4,)), dma((28,)), dma((28,)),
+            dma((5,)), dma((5,)), dma((4,)), dma((4,)), dma((36,)), dma((36,)),
             dma((8,)), dma((8,)), dma((4,)), dma((8,)), dma((8,)), dma((16,)),
         ],
         compiler_params=pltpu.CompilerParams(

time: 145 us -> 142 us (0.979)
  Pallas kernels: 137 us -> 133 us
    pallas_call x1, Pallas kernels: 137 us -> 133 us  [body(): pl.pallas_call(kernel, name='fused_step', out_shape=tuple((pltpu.VMEM(r.s...]
where the time goes in v3:
time: 142 us; the launch traced here: 139 us
  Pallas kernels  133 us (94%)
  local copies, waits for them, and re-layouts  5.88 us (4%)
    pallas_call x1, Pallas kernels, body(): pl.pallas_call(kernel, name='fused_step', out_shape=tuple((pltpu.VMEM(r.s...  133 us
    unnamed x5, local copies, waits for them, and re-layouts  5.88 us

profile of v3, /device:TPU:0, one launch (start us, length us, event | category | flops | bytes accessed | tf_op | source)
XLA Modules:
  0.0 139.5 jit_solution(17027547579210723292)
XLA Ops:
  0.6 133.0 %fused_step.1 = (f32[256,1920]{1,0:T(8,128)S(1)}, f32[256,1920]{1,0:T(8,128)S(1)}, f32[256,1920]{1,0:T(8,128)S(1)}, f32[256,1920]{1,0:T(8,128)S(1)}, bf16[512,512]{1,0:T(8,128)(2,1)S(1)}) custom-call(bf16[256,4096]{1,0:T(8,128)(2,1)} %og_hbm.1, bf16[256,1920]{1,0:T(8,128)(2,1)} %hid_hbm.1, f32[1,8]{1,0:T(1,128)} %bitcast.2, s32[1,8]{1,0:T(1,128)} %pair_ref.1, ...), custom_call_target="tpu_custom_call" | custom-call | tf_op jit(solution)/shard_map/fused_step/pallas_call | solution.py:608
  133.6 1.3 copy.19
  134.9 0.8 copy.23
  135.7 1.3 copy.20
  137.0 1.3 copy.21
  138.2 1.3 copy.22

commit v4 on v3

--- a/solution.py
+++ b/solution.py
@@ -21,7 +21,7 @@
 FL = 1920
 BLK = 256
 HALF = 128
-CHUNKS = ((0, 384), (384, 512), (896, 512), (1408, 384), (1792, 128))
+CHUNKS = ((0, 256), (256, 512), (768, 640), (1408, 384), (1792, 128))
 UNIT = 64
 
 

time: 142 us -> 144 us (1.014)
  Pallas kernels: 133 us -> 135 us
    pallas_call x1, Pallas kernels: 133 us -> 135 us  [body(): pl.pallas_call(kernel, name='fused_step', out_shape=tuple((pltpu.VMEM(r.s...]
where the time goes in v4:
time: 144 us; the launch traced here: 142 us
  Pallas kernels  135 us (94%)
  local copies, waits for them, and re-layouts  5.88 us (4%)
    pallas_call x1, Pallas kernels, body(): pl.pallas_call(kernel, name='fused_step', out_shape=tuple((pltpu.VMEM(r.s...  135 us
    unnamed x5, local copies, waits for them, and re-layouts  5.88 us

profile of v4, /device:TPU:0, one launch (start us, length us, event | category | flops | bytes accessed | tf_op | source)
XLA Modules:
  0.0 141.6 jit_solution(5779559334960599083)
XLA Ops:
  0.6 135.0 %fused_step.1 = (f32[256,1920]{1,0:T(8,128)S(1)}, f32[256,1920]{1,0:T(8,128)S(1)}, f32[256,1920]{1,0:T(8,128)S(1)}, f32[256,1920]{1,0:T(8,128)S(1)}, bf16[512,512]{1,0:T(8,128)(2,1)S(1)}) custom-call(bf16[256,4096]{1,0:T(8,128)(2,1)} %og_hbm.1, bf16[256,1920]{1,0:T(8,128)(2,1)} %hid_hbm.1, f32[1,8]{1,0:T(1,128)} %bitcast.2, s32[1,8]{1,0:T(1,128)} %pair_ref.1, ...), custom_call_target="tpu_custom_call" | custom-call | tf_op jit(solution)/shard_map/fused_step/pallas_call | solution.py:608
  135.7 1.3 copy.19
  137.0 0.8 copy.23
  137.8 1.3 copy.20
  139.0 1.3 copy.21
  140.3 1.3 copy.22
